TPU v7x, 128 devices: a whole 4x4x4 slice. The times are simulated.
128 devices in a mesh: seq: 4 (over x), dec: 32 (over y, z, core).
Axes of the slice: x: 4, y: 4, z: 4, core: 2. Of those that a mesh axis runs over, the one named last changes fastest.
Arguments:
- latents: bfloat16 [4, 4, 3, 32, 1024], P('seq', None, None, 'dec'), may hold values from -6 to 6
- cache_lat: bfloat16 [4, 4, 3, 32, 512], P('seq', None, None, 'dec'), may hold values from -6 to 6
- cache_act: bfloat16 [4, 4, 3, 32, 12288], P('seq', None, None, 'dec'), may hold values from -0.25 to 2
- w_in: bfloat16 [27, 16, 384], replicated, may hold values from -0.3125 to 0.3125
- w_mid: bfloat16 [27, 384, 384], replicated, may hold values from -0.0625 to 0.0625
- norm_gain: float32 [384], replicated, may hold values from 0.1 to 1.9
- clip_group: int32 [4, 4], replicated, may hold values from 0 to 3, as said below
- band_rows: int32 [4, 32], replicated, may hold values from 2 to 24, as said below
Outputs:
- decoded: bfloat16 [4, 32, 24, 4, 16, 384], P('seq', 'dec')
Inputs may be any that keep to these rules, and one draw needn't show every extreme that they name: For every sequence shard s, clip_group[s, :] names each of the 4 groups once. Each row of band_rows sums to 384; every band has 2 rows or more, and in each row one band has exactly 24 rows.
All inputs are finite; a program needn't handle non-finite values.
Results may differ from a plain program's by a relative error of at most 0.0029.
Values may be sent and summed in bfloat16 or wider, within the bound.
A program may use at most 192 MiB of HBM per device.

v0:
```python
import jax
import jax.numpy as jnp
from jax import lax
from jax.experimental import pallas as pl
from jax.experimental.pallas import tpu as pltpu
from jax.sharding import PartitionSpec as P

F = 4
CT = 2
COLS = 16
ZC = 16
C = 384
FRAMES = F + CT
PAD_FRAMES = 8
ROW = F * COLS
BAND = 24
EXT = BAND + 4
MID = BAND + 2
LANES = 128
EPSILON = 1e-06
MESH = pl.DeviceIdType.MESH


def band_start(band_rows, group, owner, owners):
    return lax.fori_loop(
        0,
        owners,
        lambda o, total: total + jnp.where(o < owner, band_rows[group, o], 0),
        jnp.int32(0),
    )


def exchange(
    clip_group,
    band_rows,
    lat,
    act,
    got_lat,
    got_act,
    clip_lat,
    clip_act,
    stack_lat,
    stack_act,
    slot_lat,
    slot_act,
    send_one,
    recv_one,
    send_two,
    recv_two,
):
    groups = lax.axis_size("seq")
    owners = lax.axis_size("dec")
    seq_at = lax.axis_index("seq")
    dec_at = lax.axis_index("dec")
    per_owner = lat.shape[1]

    barrier = pltpu.get_barrier_semaphore()
    for step in range(1, groups):
        pl.semaphore_signal(
            barrier,
            inc=1,
            device_id=(lax.rem(seq_at + step, groups), dec_at),
            device_id_type=MESH,
        )

    def greet(step, carry):
        pl.semaphore_signal(
            barrier,
            inc=1,
            device_id=(seq_at, lax.rem(dec_at + step, owners)),
            device_id_type=MESH,
        )
        return carry

    lax.fori_loop(1, owners, greet, 0)

    for group in range(groups):
        clip = jnp.int32(0)
        for i in range(groups):
            clip = clip + jnp.where(clip_group[seq_at, i] == group, i, 0)
        clip = jnp.minimum(clip, groups - 1)
        clip_lat[group] = lat[clip]
        clip_act[group] = act[clip]
    stack_lat[seq_at] = clip_lat[seq_at]
    stack_act[seq_at] = clip_act[seq_at]
    pl.semaphore_wait(barrier, groups - 1 + owners - 1)

    def to_group(step, which):
        group = lax.rem(seq_at + step, groups)
        source, target = ((clip_lat, stack_lat), (clip_act, stack_act))[which]
        return pltpu.make_async_remote_copy(
            src_ref=source.at[group],
            dst_ref=target.at[seq_at],
            send_sem=send_one.at[which, step],
            recv_sem=recv_one.at[which, step],
            device_id=(group, dec_at),
            device_id_type=MESH,
        )

    for which in range(2):
        for step in range(1, groups):
            to_group(step, which).start()

    def held_row(owner, start):
        first = lax.shift_right_arithmetic(start - 2 - dec_at + owners - 1, 5)
        return jnp.clip(first, 0, groups * per_owner - 1)

    def to_owner(step, which):
        owner = lax.rem(dec_at + step, owners)
        source, target = ((slot_lat, got_lat), (slot_act, got_act))[which]
        return pltpu.make_async_remote_copy(
            src_ref=source.at[owner],
            dst_ref=target.at[dec_at],
            send_sem=send_two.at[which, step],
            recv_sem=recv_two.at[which, step],
            device_id=(seq_at, owner),
            device_id_type=MESH,
        )

    for which in range(2):
        for step in range(1, groups):
            to_group(step, which).wait_recv()
        stack, slot, got = (
            (stack_lat, slot_lat, got_lat),
            (stack_act, slot_act, got_act),
        )[which]

        def fill(owner, start, stack=stack, slot=slot):
            row = held_row(owner, start)
            slot[owner] = stack[row // per_owner, lax.rem(row, per_owner)]
            return start + band_rows[seq_at, owner]

        lax.fori_loop(0, owners, fill, jnp.int32(0))
        got[dec_at] = slot[dec_at]

        def launch(step, carry, which=which):
            to_owner(step, which).start()
            return carry

        lax.fori_loop(1, owners, launch, 0)
    for which in range(2):
        for step in range(1, groups):
            to_group(step, which).wait_send()

        def finish(step, carry, which=which):
            to_owner(step, which).wait()
            return carry

        lax.fori_loop(1, owners, finish, 0)


def first_stage(start, got_lat, w_in, gain, wide, spread, taps, w_first, first_out):
    w_first[...] = jnp.zeros_like(w_first)
    for time_tap in range(3):
        for row_tap in range(3):
            at = row_tap * 256 + time_tap * 64
            w_first[at : at + 48, :] = w_in[time_tap * 3 + row_tap]

    lane = lax.broadcasted_iota(jnp.int32, (PAD_FRAMES, LANES), 1)
    spread[EXT] = jnp.zeros((PAD_FRAMES * COLS, LANES), jnp.float32)

    def columns(j, carry):
        frames = got_lat[(start - 2 + j) & 31].astype(jnp.float32)
        for col in range(COLS):
            turned = pltpu.roll(frames, (-(ZC * (col - 1))) % (COLS * ZC), 1)[:, :LANES]
            low = ZC if col == 0 else 0
            high = 2 * ZC if col == COLS - 1 else 3 * ZC
            keep = (lane >= low) & (lane < high)
            spread[j, pl.ds(col, PAD_FRAMES, stride=COLS), :] = jnp.where(keep, turned, 0.0)
        return carry

    lax.fori_loop(0, EXT, columns, 0)

    def pair(j, carry):
        here = spread[j]
        after = pltpu.roll(here, 64, 1)
        count = FRAMES * COLS
        taps[j] = (here[:count] + after[COLS : COLS + count]).astype(jnp.bfloat16)
        return carry

    lax.fori_loop(0, EXT + 1, pair, 0)

    rows = MID // 2
    for part in range(2):
        blocks = []
        for r in range(rows):
            j = part * rows + r + 1
            height = lax.rem(start - 2 + j + 96, 96)
            picks = (
                jnp.where(height == 0, EXT, j - 1),
                j,
                jnp.where(height == 95, EXT, j + 1),
            )
            pieces = []
            for pick in picks:
                block = taps[pick]
                pieces += [block[:ROW], block[2 * COLS : 2 * COLS + ROW]]
            blocks.append(jnp.concatenate(pieces, axis=1))
        slab = jnp.concatenate(blocks, axis=0)
        total = jnp.dot(slab, w_first[...], preferred_element_type=jnp.float32)
        first_out[part * rows : (part + 1) * rows] = total.reshape(rows, ROW, C)


def shifted(values, position):
    count = values.shape[0]
    before = jnp.where(position == 0, 0.0, pltpu.roll(values, 1, 0))
    after = jnp.where(position == COLS - 1, 0.0, pltpu.roll(values, count - 1, 0))
    return jnp.concatenate([before, values, after], axis=1).astype(jnp.bfloat16)


def cache_stage(start, got_act, conv_in):
    position = lax.broadcasted_iota(jnp.int32, (CT * COLS, C), 0) & (COLS - 1)

    def one(i, carry):
        values = got_act[(start - 1 + i) & 31].astype(jnp.float32)
        conv_in[i, : CT * COLS] = shifted(values, position)
        return carry

    lax.fori_loop(0, MID, one, 0)


def act_stage(gain, first_out, conv_in):
    position = lax.broadcasted_iota(jnp.int32, (ROW, C), 0) & (COLS - 1)
    conv_in[MID] = jnp.zeros((FRAMES * COLS, 3 * C), jnp.bfloat16)

    def one(i, carry):
        values = first_out[i]
        mean = jnp.mean(values * values, axis=1, keepdims=True)
        scaled = values * lax.rsqrt(mean + EPSILON) * gain[...]
        conv_in[i, CT * COLS :] = shifted(scaled / (1.0 + jnp.exp(-scaled)), position)
        return carry

    lax.fori_loop(0, MID, one, 0)


def second_stage(start, live, w_mid, first_out, conv_in, out, chunk):
    def rows_from(part, carry):
        base = part * chunk
        total = jnp.zeros((chunk * ROW, C), jnp.float32)
        for row_tap in range(3):
            picks = []
            for r in range(chunk):
                height = lax.rem(start + base + r, 96)
                pick = base + r + row_tap
                if row_tap == 0:
                    pick = jnp.where(height == 0, MID, pick)
                if row_tap == 2:
                    pick = jnp.where(height == 95, MID, pick)
                picks.append(pick)
            for time_tap in range(3):
                at = time_tap * COLS
                slab = jnp.concatenate(
                    [conv_in[pick, at : at + ROW, :] for pick in picks], axis=0
                )
                total = total + jnp.dot(
                    slab, w_mid[time_tap * 3 + row_tap], preferred_element_type=jnp.float32
                )
        for r in range(chunk):
            value = total[r * ROW : (r + 1) * ROW] + first_out[base + r + 1]
            out[base + r] = jnp.where(base + r < live, value, 0.0).astype(jnp.bfloat16)
        return carry

    lax.fori_loop(0, BAND // chunk, rows_from, 0)


def convolve(
    place,
    band_rows,
    got_lat,
    got_act,
    w_in,
    w_mid,
    gain,
    out,
    wide,
    spread,
    taps,
    w_first,
    first_out,
    conv_in,
):
    group, owner = place[0], place[1]
    start = band_start(band_rows, group, owner, band_rows.shape[1])
    live = band_rows[group, owner]
    cache_stage(start, got_act, conv_in)
    first_stage(start, got_lat, w_in, gain, wide, spread, taps, w_first, first_out)
    act_stage(gain, first_out, conv_in)
    second_stage(start, live, w_mid, first_out, conv_in, out, 8)


VM = pl.BlockSpec(memory_space=pltpu.VMEM)
SM = pl.BlockSpec(memory_space=pltpu.SMEM)


def run_convolve(place, band_rows, got_lat, got_act, w_in, w_mid, gain):
    return pl.pallas_call(
        convolve,
        out_shape=jax.ShapeDtypeStruct((BAND, ROW, C), jnp.bfloat16),
        in_specs=[SM, SM, VM, VM, VM, VM, VM],
        out_specs=VM,
        scratch_shapes=[
            pltpu.VMEM((8, 128), jnp.float32),
            pltpu.VMEM((EXT + 1, PAD_FRAMES * COLS, LANES), jnp.float32),
            pltpu.VMEM((EXT + 1, FRAMES * COLS, LANES), jnp.bfloat16),
            pltpu.VMEM((768, C), jnp.bfloat16),
            pltpu.VMEM((MID, ROW, C), jnp.float32),
            pltpu.VMEM((MID + 1, FRAMES * COLS, 3 * C), jnp.bfloat16),
        ],
        compiler_params=pltpu.CompilerParams(vmem_limit_bytes=48 << 20),
        name="convolve",
    )(place, band_rows, got_lat, got_act, w_in, w_mid, gain)


def run_exchange(clip_group, band_rows, lat, act):
    groups = lax.axis_size("seq")
    owners = lax.axis_size("dec")
    per_owner = lat.shape[1]
    lat_row, act_row = lat.shape[2:], act.shape[2:]
    bf16 = jnp.bfloat16
    return pl.pallas_call(
        exchange,
        out_shape=(
            jax.ShapeDtypeStruct((owners,) + lat_row, bf16),
            jax.ShapeDtypeStruct((owners,) + act_row, bf16),
        ),
        in_specs=[SM, SM, VM, VM],
        out_specs=(VM, VM),
        scratch_shapes=[
            pltpu.VMEM((groups, per_owner) + lat_row, bf16),
            pltpu.VMEM((groups, per_owner) + act_row, bf16),
            pltpu.VMEM((groups, per_owner) + lat_row, bf16),
            pltpu.VMEM((groups, per_owner) + act_row, bf16),
            pltpu.VMEM((owners,) + lat_row, bf16),
            pltpu.VMEM((owners,) + act_row, bf16),
            pltpu.SemaphoreType.DMA((2, groups)),
            pltpu.SemaphoreType.DMA((2, groups)),
            pltpu.SemaphoreType.DMA((2, owners)),
            pltpu.SemaphoreType.DMA((2, owners)),
        ],
        compiler_params=pltpu.CompilerParams(
            collective_id=0, has_side_effects=True, vmem_limit_bytes=16 << 20
        ),
        name="exchange",
    )(clip_group, band_rows, lat, act)


def shards(latents, cache_lat, cache_act, w_in, w_mid, norm_gain, clip_group, band_rows):
    groups, per_owner = latents.shape[1], latents.shape[2]
    new_lat = latents.reshape(groups, per_owner, F, COLS * ZC)
    old_lat = cache_lat.reshape(groups, per_owner, CT, COLS * ZC)
    lat = jnp.concatenate([old_lat, new_lat, jnp.zeros_like(old_lat)], axis=2)
    act = cache_act.reshape(groups, per_owner, CT * COLS, C)
    got_lat, got_act = run_exchange(clip_group, band_rows, lat, act)
    place = jnp.stack([lax.axis_index("seq"), lax.axis_index("dec")]).astype(jnp.int32)
    out = run_convolve(
        place,
        band_rows,
        got_lat,
        got_act,
        w_in.reshape(9, 3 * ZC, C),
        w_mid.reshape(9, 3 * C, C),
        norm_gain.reshape(1, C),
    )
    return out.reshape(1, 1, BAND, F, COLS, C)


def solution(mesh):
    placed = P("seq", None, None, "dec", None)
    return jax.shard_map(
        shards,
        mesh=mesh,
        in_specs=(placed, placed, placed, P(), P(), P(), P(), P()),
        out_specs=P("seq", "dec", None, None, None, None),
        check_vma=False,
    )
```

profile of v0, /device:TPU:1, one launch (start us, length us, event | category | flops | bytes accessed | tf_op | source)
XLA Modules:
  0.0 67.9 jit_solution(14128568055369413994)
XLA Ops:
  0.0 0.1 pad_add_fusion.place
  0.1 0.1 pad.2.clone
  0.2 0.7 %reshape.26.gain = f32[1,384]{1,0:T(1,128)S(1)} reshape(f32[384]{0:T(512)} %param.13) | data formatting | bytes 3072 | tf_op jit(solution)/shard_map/reshape | solution.py:362
  0.8 0.7 %reshape.21 = bf16[4,3,2,256]{3,2,0,1:T(2,128)(2,1)S(1)} reshape(bf16[1,4,3,1,512]{4,1,3,2,0:T(4,128)(2,1)} %param.9) | data formatting | bytes 24576 | tf_op jit(solution)/shard_map/reshape | solution.py:350
  1.6 0.8 %reshape.22 = bf16[4,3,4,256]{3,2,0,1:T(4,128)(2,1)S(1)} reshape(bf16[1,4,3,1,1024]{4,1,3,2,0:T(4,128)(2,1)} %param.8) | data formatting | bytes 49152 | tf_op jit(solution)/shard_map/reshape | solution.py:349
  2.3 0.1 maximum_maximum_fusion.lat
  2.4 1.1 %reshape.23 = bf16[4,3,32,384]{3,2,0,1:T(8,128)(2,1)S(1)} reshape(bf16[1,4,3,1,12288]{4,1,3,2,0:T(4,128)(2,1)} %param.10) | data formatting | bytes 589824 | tf_op jit(solution)/shard_map/reshape | solution.py:352
  3.6 0.0 copy-start.1
  3.6 0.7 copy-done.1
  4.3 0.0 copy-start.3
  4.3 0.7 %copy-done.3 = s32[4,4]{1,0:T(4,128)S(1)} copy-done((s32[4,4]{1,0:T(4,128)S(1)}, s32[4,4]{1,0:T(4,128)}, u32[]{:S(2)}) %copy-start.3) | copy-done | bytes 88
  5.0 27.9 %exchange.1 = (bf16[32,8,256]{2,1,0:T(8,128)(2,1)S(1)}, bf16[32,32,384]{2,1,0:T(8,128)(2,1)S(1)}) custom-call(s32[4,4]{1,0:T(4,128)S(1)} %copy-done.3, s32[4,32]{1,0:T(4,128)S(1)} %copy-done.1, bf16[4,3,8,256]{3,2,1,0:T(8,128)(2,1)S(1)} %maximum_maximum_fusion.lat, bf16[4,3,32,384]{3,2,1,0:T(8,128)(2,1)S(1)} %copy.14.act), custom_call_target="tpu_custom_call" | custom-call | tf_op jit(solution)/shard_map/exchange/pallas_call | solution.py:320
  32.8 0.0 copy-start
  32.8 1.0 %copy-done = bf16[27,16,384]{2,1,0:T(8,128)(2,1)S(1)} copy-done((bf16[27,16,384]{2,1,0:T(8,128)(2,1)S(1)}, bf16[27,16,384]{2,1,0:T(8,128)(2,1)}, u32[]{:S(2)}) %copy-start) | copy-done | bytes 331800
  33.8 0.0 copy-start.2
  33.8 0.7 %copy-done.2 = s32[4,32]{1,0:T(4,128)S(1)} copy-done((s32[4,32]{1,0:T(4,128)S(1)}, s32[4,32]{1,0:T(4,128)}, u32[]{:S(2)}) %copy-start.2) | copy-done | bytes 536
  34.5 33.4 %convolve.1 = bf16[24,64,384]{2,1,0:T(8,128)(2,1)} custom-call(s32[2]{0:T(128)S(1)} %pad_add_fusion.place, s32[4,32]{1,0:T(4,128)S(1)} %copy-done.2, bf16[32,8,256]{2,1,0:T(8,128)(2,1)S(1)} %get-tuple-element.7.got_lat, bf16[32,32,384]{2,1,0:T(8,128)(2,1)S(1)} %get-tuple-element.8.got_act, bf16[9,48,384]{2,1,0:T(8,128)(2,1)S(1)} %bitcast.11, ...), custom_call_target="tpu_custom_call" | custom-call | tf_op jit(solution)/shard_map/convolve/pallas_call | solution.py:296
  (2 shorter events, 0.0 us)
Async XLA Ops:
  3.6 0.7 %copy-start.1 = (s32[4,32]{1,0:T(4,128)S(1)}, s32[4,32]{1,0:T(4,128)}, u32[]{:S(2)}) copy-start(s32[4,32]{1,0:T(4,128)} %band_rows.3) | copy-start | bytes 1540
  4.3 0.7 %copy-start.3 = (s32[4,4]{1,0:T(4,128)S(1)}, s32[4,4]{1,0:T(4,128)}, u32[]{:S(2)}) copy-start(s32[4,4]{1,0:T(4,128)} %clip_group.1) | copy-start | bytes 196
  32.8 1.0 %copy-start = (bf16[27,16,384]{2,1,0:T(8,128)(2,1)S(1)}, bf16[27,16,384]{2,1,0:T(8,128)(2,1)}, u32[]{:S(2)}) copy-start(bf16[27,16,384]{2,1,0:T(8,128)(2,1)} %param.11) | copy-start | bytes 995332
  33.8 0.7 %copy-start.2 = (s32[4,32]{1,0:T(4,128)S(1)}, s32[4,32]{1,0:T(4,128)}, u32[]{:S(2)}) copy-start(s32[4,32]{1,0:T(4,128)} %band_rows.3) | copy-start | bytes 1540
where the time goes:
time: 68.6 us; the launch traced here: 67.9 us
  Pallas kernels  61.3 us (89%)
  local copies, waits for them, and re-layouts  6.42 us (9%)
    pallas_call x1, Pallas kernels, run_convolve(): pl.pallas_call(convolve, out_shape=jax.ShapeDtypeStruct((BAND, ROW, C), j...  33.4 us
    pallas_call x1, Pallas kernels, run_exchange(): pl.pallas_call(exchange, out_shape=(jax.ShapeDtypeStruct((owners,) + lat_...  27.9 us
    unnamed x8, local copies, waits for them, and re-layouts  3.01 us

commit v1 on v0

v1 whole, which is shorter than its diff:
```python
import jax
import jax.numpy as jnp
from jax import lax
from jax.experimental import pallas as pl
from jax.experimental.pallas import tpu as pltpu
from jax.sharding import PartitionSpec as P

F = 4
CT = 2
COLS = 16
ZC = 16
C = 384
FRAMES = F + CT
PAD_FRAMES = 8
ROW = F * COLS
BAND = 24
EXT = BAND + 4
MID = BAND + 2
LANES = 128
EPSILON = 1e-06
MESH = pl.DeviceIdType.MESH


def band_start(band_rows, group, owner, owners):
    return lax.fori_loop(
        0,
        owners,
        lambda o, total: total + jnp.where(o < owner, band_rows[group, o], 0),
        jnp.int32(0),
    )


def first_stage(start, got_lat, spread, taps, w_first, first_out):
    lane = lax.broadcasted_iota(jnp.int32, (PAD_FRAMES, LANES), 1)
    spread[EXT] = jnp.zeros((PAD_FRAMES * COLS, LANES), jnp.float32)

    def columns(j, carry):
        frames = got_lat[(start - 2 + j) & 31].astype(jnp.float32)
        for col in range(COLS):
            turned = pltpu.roll(frames, (-(ZC * (col - 1))) % (COLS * ZC), 1)[:, :LANES]
            low = ZC if col == 0 else 0
            high = 2 * ZC if col == COLS - 1 else 3 * ZC
            keep = (lane >= low) & (lane < high)
            spread[j, pl.ds(col, PAD_FRAMES, stride=COLS), :] = jnp.where(keep, turned, 0.0)
        return carry

    lax.fori_loop(0, EXT, columns, 0)

    def pair(j, carry):
        here = spread[j]
        after = pltpu.roll(here, 64, 1)
        count = FRAMES * COLS
        taps[j] = (here[:count] + after[COLS : COLS + count]).astype(jnp.bfloat16)
        return carry

    lax.fori_loop(0, EXT + 1, pair, 0)

    rows = MID // 2
    for part in range(2):
        blocks = []
        for r in range(rows):
            j = part * rows + r + 1
            height = lax.rem(start - 2 + j + 96, 96)
            picks = (
                jnp.where(height == 0, EXT, j - 1),
                j,
                jnp.where(height == 95, EXT, j + 1),
            )
            pieces = []
            for pick in picks:
                block = taps[pick]
                pieces += [block[:ROW], block[2 * COLS : 2 * COLS + ROW]]
            blocks.append(jnp.concatenate(pieces, axis=1))
        slab = jnp.concatenate(blocks, axis=0)
        total = jnp.dot(slab, w_first[...], preferred_element_type=jnp.float32)
        first_out[part * rows : (part + 1) * rows] = total.reshape(rows, ROW, C)


def shifted(values, position):
    count = values.shape[0]
    before = jnp.where(position == 0, 0.0, pltpu.roll(values, 1, 0))
    after = jnp.where(position == COLS - 1, 0.0, pltpu.roll(values, count - 1, 0))
    return jnp.concatenate([before, values, after], axis=1).astype(jnp.bfloat16)


def cache_stage(start, got_act, conv_in):
    position = lax.broadcasted_iota(jnp.int32, (CT * COLS, C), 0) & (COLS - 1)

    def one(i, carry):
        values = got_act[(start - 1 + i) & 31].astype(jnp.float32)
        conv_in[i, : CT * COLS] = shifted(values, position)
        return carry

    lax.fori_loop(0, MID, one, 0)


def act_stage(gain, first_out, conv_in):
    position = lax.broadcasted_iota(jnp.int32, (ROW, C), 0) & (COLS - 1)
    conv_in[MID] = jnp.zeros((FRAMES * COLS, 3 * C), jnp.bfloat16)

    def one(i, carry):
        values = first_out[i]
        mean = jnp.mean(values * values, axis=1, keepdims=True)
        scaled = values * lax.rsqrt(mean + EPSILON) * gain[...]
        conv_in[i, CT * COLS :] = shifted(scaled / (1.0 + jnp.exp(-scaled)), position)
        return carry

    lax.fori_loop(0, MID, one, 0)


def tap_rows(start, row):
    height = lax.rem(start + row, 96)
    return (
        jnp.where(height == 0, MID, row),
        row + 1,
        jnp.where(height == 95, MID, row + 2),
    )


def tap_sum(start, base, count, time_tap, low, high, w_mid, conv_in):
    at = (low + time_tap) * COLS
    size = (high - low) * COLS
    blocks = []
    for r in range(count):
        picks = tap_rows(start, base + r)
        blocks.append(
            jnp.concatenate([conv_in[pick, at : at + size, :] for pick in picks], axis=1)
        )
    slab = jnp.concatenate(blocks, axis=0)
    return jnp.dot(slab, w_mid[time_tap], preferred_element_type=jnp.float32)


def second_new(start, w_mid, first_out, conv_in, chunk):
    def some(part, carry):
        base = part * chunk
        for time_tap in range(3):
            low = CT - time_tap
            size = (F - low) * COLS
            total = tap_sum(start, base, chunk, time_tap, low, F, w_mid, conv_in)
            for r in range(chunk):
                first_out[base + r + 1, low * COLS :] += total[r * size : (r + 1) * size]
        return carry

    lax.fori_loop(0, BAND // chunk, some, 0)


def second_old(start, live, w_mid, first_out, conv_in, out, chunk):
    def some(part, carry):
        base = part * chunk
        for time_tap in range(CT):
            size = (CT - time_tap) * COLS
            total = tap_sum(start, base, chunk, time_tap, 0, CT - time_tap, w_mid, conv_in)
            for r in range(chunk):
                first_out[base + r + 1, :size] += total[r * size : (r + 1) * size]
        for r in range(chunk):
            value = first_out[base + r + 1]
            out[base + r] = jnp.where(base + r < live, value, 0.0).astype(jnp.bfloat16)
        return carry

    lax.fori_loop(0, BAND // chunk, some, 0)


def block(
    clip_group,
    band_rows,
    lat,
    act,
    gain,
    w_in,
    w_mid,
    out,
    got_lat,
    got_act,
    clip_lat,
    clip_act,
    stack_lat,
    stack_act,
    slot_lat,
    slot_act,
    w_first,
    w_second,
    spread,
    taps,
    first_out,
    conv_in,
    send_one,
    recv_one,
    send_two,
    recv_two,
    load,
):
    groups = lax.axis_size("seq")
    owners = lax.axis_size("dec")
    seq_at = lax.axis_index("seq")
    dec_at = lax.axis_index("dec")
    per_owner = lat.shape[1]

    barrier = pltpu.get_barrier_semaphore()
    for step in range(1, groups):
        pl.semaphore_signal(
            barrier,
            inc=1,
            device_id=(lax.rem(seq_at + step, groups), dec_at),
            device_id_type=MESH,
        )

    def greet(step, carry):
        pl.semaphore_signal(
            barrier,
            inc=1,
            device_id=(seq_at, lax.rem(dec_at + step, owners)),
            device_id_type=MESH,
        )
        return carry

    lax.fori_loop(1, owners, greet, 0)

    for group in range(groups):
        clip = jnp.int32(0)
        for i in range(groups):
            clip = clip + jnp.where(clip_group[seq_at, i] == group, i, 0)
        clip = jnp.minimum(clip, groups - 1)
        clip_lat[group] = lat[clip]
        clip_act[group] = act[clip]
    stack_lat[seq_at] = clip_lat[seq_at]
    stack_act[seq_at] = clip_act[seq_at]
    w_first[...] = jnp.zeros_like(w_first)
    pl.semaphore_wait(barrier, groups - 1 + owners - 1)

    def to_group(step, which):
        group = lax.rem(seq_at + step, groups)
        source, target = ((clip_lat, stack_lat), (clip_act, stack_act))[which]
        return pltpu.make_async_remote_copy(
            src_ref=source.at[group],
            dst_ref=target.at[seq_at],
            send_sem=send_one.at[which, step],
            recv_sem=recv_one.at[which, step],
            device_id=(group, dec_at),
            device_id_type=MESH,
        )

    for which in range(2):
        for step in range(1, groups):
            to_group(step, which).start()

    loads = [pltpu.make_async_copy(w_mid, w_second, load.at[9])]
    for time_tap in range(3):
        for row_tap in range(3):
            tap = time_tap * 3 + row_tap
            at = row_tap * 256 + time_tap * 64
            loads.append(
                pltpu.make_async_copy(
                    w_in.at[tap], w_first.at[at : at + 3 * ZC, :], load.at[tap]
                )
            )
    for copy in loads[1:] + loads[:1]:
        copy.start()

    def held_row(owner, start):
        first = lax.shift_right_arithmetic(start - 2 - dec_at + owners - 1, 5)
        return jnp.clip(first, 0, groups * per_owner - 1)

    def to_owner(step, which):
        owner = lax.rem(dec_at + step, owners)
        source, target = ((slot_lat, got_lat), (slot_act, got_act))[which]
        return pltpu.make_async_remote_copy(
            src_ref=source.at[owner],
            dst_ref=target.at[dec_at],
            send_sem=send_two.at[which, step],
            recv_sem=recv_two.at[which, step],
            device_id=(seq_at, owner),
            device_id_type=MESH,
        )

    def pass_on(which):
        stack, slot, got = (
            (stack_lat, slot_lat, got_lat),
            (stack_act, slot_act, got_act),
        )[which]
        for step in range(1, groups):
            to_group(step, which).wait_recv()

        def fill(owner, start):
            row = held_row(owner, start)
            slot[owner] = stack[row // per_owner, lax.rem(row, per_owner)]
            return start + band_rows[seq_at, owner]

        lax.fori_loop(0, owners, fill, jnp.int32(0))
        got[dec_at] = slot[dec_at]

        def launch(step, carry):
            to_owner(step, which).start()
            return carry

        lax.fori_loop(1, owners, launch, 0)

    def collect(which):
        def arrive(step, carry):
            to_owner(step, which).wait_recv()
            return carry

        lax.fori_loop(1, owners, arrive, 0)

    start = band_start(band_rows, seq_at, dec_at, owners)
    live = band_rows[seq_at, dec_at]
    pass_on(0)
    pass_on(1)
    collect(0)
    for copy in loads[1:]:
        copy.wait()
    first_stage(start, got_lat, spread, taps, w_first, first_out)
    act_stage(gain, first_out, conv_in)
    loads[0].wait()
    second_new(start, w_second, first_out, conv_in, 8)
    collect(1)
    cache_stage(start, got_act, conv_in)
    second_old(start, live, w_second, first_out, conv_in, out, 24)

    for which in range(2):
        for step in range(1, groups):
            to_group(step, which).wait_send()

        def finish(step, carry, which=which):
            to_owner(step, which).wait_send()
            return carry

        lax.fori_loop(1, owners, finish, 0)


def run_block(clip_group, band_rows, lat, act, gain, w_in, w_mid):
    groups = lax.axis_size("seq")
    owners = lax.axis_size("dec")
    per_owner = lat.shape[1]
    lat_row, act_row = lat.shape[2:], act.shape[2:]
    bf16 = jnp.bfloat16
    vm = pl.BlockSpec(memory_space=pltpu.VMEM)
    sm = pl.BlockSpec(memory_space=pltpu.SMEM)
    hbm = pl.BlockSpec(memory_space=pl.ANY)
    return pl.pallas_call(
        block,
        out_shape=jax.ShapeDtypeStruct((BAND, ROW, C), bf16),
        in_specs=[sm, sm, vm, vm, vm, hbm, hbm],
        out_specs=vm,
        scratch_shapes=[
            pltpu.VMEM((owners,) + lat_row, bf16),
            pltpu.VMEM((owners,) + act_row, bf16),
            pltpu.VMEM((groups, per_owner) + lat_row, bf16),
            pltpu.VMEM((groups, per_owner) + act_row, bf16),
            pltpu.VMEM((groups, per_owner) + lat_row, bf16),
            pltpu.VMEM((groups, per_owner) + act_row, bf16),
            pltpu.VMEM((owners,) + lat_row, bf16),
            pltpu.VMEM((owners,) + act_row, bf16),
            pltpu.VMEM((768, C), bf16),
            pltpu.VMEM(w_mid.shape, bf16),
            pltpu.VMEM((EXT + 1, PAD_FRAMES * COLS, LANES), jnp.float32),
            pltpu.VMEM((EXT + 1, FRAMES * COLS, LANES), bf16),
            pltpu.VMEM((MID, ROW, C), jnp.float32),
            pltpu.VMEM((MID + 1, FRAMES * COLS, 3 * C), bf16),
            pltpu.SemaphoreType.DMA((2, groups)),
            pltpu.SemaphoreType.DMA((2, groups)),
            pltpu.SemaphoreType.DMA((2, owners)),
            pltpu.SemaphoreType.DMA((2, owners)),
            pltpu.SemaphoreType.DMA((10,)),
        ],
        compiler_params=pltpu.CompilerParams(
            collective_id=0, has_side_effects=True, vmem_limit_bytes=52 << 20
        ),
        name="block",
    )(clip_group, band_rows, lat, act, gain, w_in, w_mid)


def shards(latents, cache_lat, cache_act, w_in, w_mid, norm_gain, clip_group, band_rows):
    groups, per_owner = latents.shape[1], latents.shape[2]
    new_lat = latents.reshape(groups, per_owner, F, COLS * ZC)
    old_lat = cache_lat.reshape(groups, per_owner, CT, COLS * ZC)
    lat = jnp.concatenate([old_lat, new_lat, jnp.zeros_like(old_lat)], axis=2)
    act = cache_act.reshape(groups, per_owner, CT * COLS, C)
    out = run_block(
        clip_group,
        band_rows,
        lat,
        act,
        norm_gain.reshape(1, C),
        w_in.reshape(9, 3 * ZC, C),
        w_mid.reshape(3, 9 * C, C),
    )
    return out.reshape(1, 1, BAND, F, COLS, C)


def solution(mesh):
    placed = P("seq", None, None, "dec", None)
    return jax.shard_map(
        shards,
        mesh=mesh,
        in_specs=(placed, placed, placed, P(), P(), P(), P(), P()),
        out_specs=P("seq", "dec", None, None, None, None),
        check_vma=False,
    )
```

time: 68.6 us -> 53.6 us (0.78)
  Pallas kernels: 61.3 us -> 48.8 us
  local copies, waits for them, and re-layouts: 6.42 us -> 4.47 us
    pallas_call x2 -> x1, Pallas kernels: 61.3 us -> 48.8 us  [run_block(): pl.pallas_call(block, out_shape=jax.ShapeDtypeStruct((BAND, ROW, C), bf16...]
    unnamed x8 -> x7, local copies, waits for them, and re-layouts: 3.01 us -> 1.03 us
where the time goes in v1:
time: 53.6 us; the launch traced here: 53.4 us
  Pallas kernels  48.8 us (91%)
  local copies, waits for them, and re-layouts  4.47 us (8%)
    pallas_call x1, Pallas kernels, run_block(): pl.pallas_call(block, out_shape=jax.ShapeDtypeStruct((BAND, ROW, C), bf16...  48.8 us
    reshape x2, local copies, waits for them, and re-layouts, shards(): act = cache_act.reshape(groups, per_owner, CT * COLS, C)  1.18 us

profile of v1, /device:TPU:1, one launch (start us, length us, event | category | flops | bytes accessed | tf_op | source)
XLA Modules:
  0.0 53.4 jit_solution(3877429875084778652)
XLA Ops:
  0.0 0.0 copy-start.2
  0.0 0.0 copy-start.1
  0.0 0.0 copy-start
  0.0 0.1 pad.2.clone
  0.1 0.7 %reshape.24.gain = f32[1,384]{1,0:T(1,128)S(1)} reshape(f32[384]{0:T(512)} %param.13) | data formatting | bytes 3072 | tf_op jit(solution)/shard_map/reshape | solution.py:383
  0.8 0.7 %reshape.21 = bf16[4,3,2,256]{3,2,0,1:T(2,128)(2,1)S(1)} reshape(bf16[1,4,3,1,512]{4,1,3,2,0:T(4,128)(2,1)} %param.9) | data formatting | bytes 24576 | tf_op jit(solution)/shard_map/reshape | solution.py:375
  1.5 0.8 %reshape.22 = bf16[4,3,4,256]{3,2,0,1:T(4,128)(2,1)S(1)} reshape(bf16[1,4,3,1,1024]{4,1,3,2,0:T(4,128)(2,1)} %param.8) | data formatting | bytes 49152 | tf_op jit(solution)/shard_map/reshape | solution.py:374
  2.3 0.1 maximum_maximum_fusion.lat
  2.4 1.1 %reshape.23 = bf16[4,3,32,384]{3,2,0,1:T(8,128)(2,1)S(1)} reshape(bf16[1,4,3,1,12288]{4,1,3,2,0:T(4,128)(2,1)} %param.10) | data formatting | bytes 589824 | tf_op jit(solution)/shard_map/reshape | solution.py:377
  3.6 0.0 copy-done.2
  3.6 0.0 copy-done.1
  3.6 0.0 copy-done
  3.6 48.8 %block.1 = bf16[24,64,384]{2,1,0:T(8,128)(2,1)S(1)} custom-call(s32[4,4]{1,0:T(4,128)S(1)} %copy-done.1, s32[4,32]{1,0:T(4,128)S(1)} %copy-done.2, bf16[4,3,8,256]{3,2,1,0:T(8,128)(2,1)S(1)} %maximum_maximum_fusion.lat, bf16[4,3,32,384]{3,2,1,0:T(8,128)(2,1)S(1)} %copy.14.act, f32[1,384]{1,0:T(1,128)S(1)} %reshape.24.gain, bf16[9,48,384]{2,1,0:T(8,128)(2,1)S(1)} %bitcast.10, ...), custom_call_target="tpu_custom_call" | custom-call | tf_op jit(solution)/shard_map/block/pallas_call | solution.py:339
  52.3 1.0 %copy.20 = bf16[1,1,24,4,16,384]{5,4,3,2,1,0:T(8,128)(2,1)} copy(bf16[1,1,24,4,16,384]{5,4,3,2,1,0:T(8,128)(2,1)S(1)} %bitcast.9) | data formatting | bytes 2359296
  (2 shorter events, 0.0 us)
Async XLA Ops:
  0.0 3.6 %copy-start.2 = (s32[4,32]{1,0:T(4,128)S(1)}, s32[4,32]{1,0:T(4,128)}, u32[]{:S(2)}) copy-start(s32[4,32]{1,0:T(4,128)} %band_rows.1) | copy-start | bytes 1540
  0.0 3.6 %copy-start.1 = (s32[4,4]{1,0:T(4,128)S(1)}, s32[4,4]{1,0:T(4,128)}, u32[]{:S(2)}) copy-start(s32[4,4]{1,0:T(4,128)} %clip_group.1) | copy-start | bytes 196
  0.0 3.6 %copy-start = (bf16[27,16,384]{2,1,0:T(8,128)(2,1)S(1)}, bf16[27,16,384]{2,1,0:T(8,128)(2,1)}, u32[]{:S(2)}) copy-start(bf16[27,16,384]{2,1,0:T(8,128)(2,1)} %param.11) | copy-start | bytes 995332

commit v2 on v1

--- a/solution.py
+++ b/solution.py
@@ -17,6 +17,7 @@
 EXT = BAND + 4
 MID = BAND + 2
 LANES = 128
+TOGETHER = 4
 EPSILON = 1e-06
 MESH = pl.DeviceIdType.MESH
 
@@ -30,30 +31,56 @@
     )
 
 
-def first_stage(start, got_lat, spread, taps, w_first, first_out):
-    lane = lax.broadcasted_iota(jnp.int32, (PAD_FRAMES, LANES), 1)
-    spread[EXT] = jnp.zeros((PAD_FRAMES * COLS, LANES), jnp.float32)
-
-    def columns(j, carry):
-        frames = got_lat[(start - 2 + j) & 31].astype(jnp.float32)
-        for col in range(COLS):
-            turned = pltpu.roll(frames, (-(ZC * (col - 1))) % (COLS * ZC), 1)[:, :LANES]
-            low = ZC if col == 0 else 0
-            high = 2 * ZC if col == COLS - 1 else 3 * ZC
-            keep = (lane >= low) & (lane < high)
-            spread[j, pl.ds(col, PAD_FRAMES, stride=COLS), :] = jnp.where(keep, turned, 0.0)
-        return carry
-
-    lax.fori_loop(0, EXT, columns, 0)
-
-    def pair(j, carry):
-        here = spread[j]
-        after = pltpu.roll(here, 64, 1)
-        count = FRAMES * COLS
-        taps[j] = (here[:count] + after[COLS : COLS + count]).astype(jnp.bfloat16)
-        return carry
-
-    lax.fori_loop(0, EXT + 1, pair, 0)
+def make_pick(pick):
+    shape = (2 * COLS * ZC, LANES)
+    source = lax.broadcasted_iota(jnp.int32, shape, 0)
+    lane = lax.broadcasted_iota(jnp.int32, shape, 1)
+    frame = source >= COLS * ZC
+    inner = jnp.where(frame, lane - 64, lane)
+    here = source & (COLS * ZC - 1)
+
+    inside = (inner >= 0) & (inner < 3 * ZC)
+
+    def some(part, carry):
+        for i in range(TOGETHER):
+            wanted = here - ZC * (part * TOGETHER + i - 1)
+            block = jnp.where(inside & (inner == wanted), 1.0, 0.0).astype(jnp.bfloat16)
+            pick[part, :, i * LANES : (i + 1) * LANES] = block
+        return carry
+
+    lax.fori_loop(0, COLS // TOGETHER, some, 0)
+
+
+def first_stage(start, got_lat, pick, pairs, spread, taps, w_first, first_out):
+    def gather(i, carry):
+        rows = []
+        for k in range(2):
+            frames = got_lat[(start - 2 + 2 * i + k) & 31].astype(jnp.float32)
+            after = pltpu.roll(frames, PAD_FRAMES - 1, 0)
+            rows.append(jnp.concatenate([frames, after], axis=1))
+        pairs[i] = jnp.concatenate(rows, axis=0).astype(jnp.bfloat16)
+        return carry
+
+    lax.fori_loop(0, EXT // 2, gather, 0)
+    source = pairs[...].reshape(EXT * PAD_FRAMES, 2 * COLS * ZC)
+
+    def columns(part, carry):
+        block = jnp.dot(source, pick[part], preferred_element_type=jnp.float32)
+        for i in range(TOGETHER):
+            col = part * TOGETHER + i
+            rows = pl.ds(col, EXT * PAD_FRAMES, stride=COLS)
+            spread[rows, :] = block[:, i * LANES : (i + 1) * LANES]
+        return carry
+
+    lax.fori_loop(0, COLS // TOGETHER, columns, 0)
+    taps[EXT] = jnp.zeros((FRAMES * COLS, LANES), jnp.bfloat16)
+
+    def narrow(j, carry):
+        at = pl.multiple_of(j * PAD_FRAMES * COLS, PAD_FRAMES * COLS)
+        taps[j] = spread[pl.ds(at, FRAMES * COLS), :].astype(jnp.bfloat16)
+        return carry
+
+    lax.fori_loop(0, EXT, narrow, 0)
 
     rows = MID // 2
     for part in range(2):
@@ -67,8 +94,8 @@
                 jnp.where(height == 95, EXT, j + 1),
             )
             pieces = []
-            for pick in picks:
-                block = taps[pick]
+            for at in picks:
+                block = taps[at]
                 pieces += [block[:ROW], block[2 * COLS : 2 * COLS + ROW]]
             blocks.append(jnp.concatenate(pieces, axis=1))
         slab = jnp.concatenate(blocks, axis=0)
@@ -97,12 +124,13 @@
 def act_stage(gain, first_out, conv_in):
     position = lax.broadcasted_iota(jnp.int32, (ROW, C), 0) & (COLS - 1)
     conv_in[MID] = jnp.zeros((FRAMES * COLS, 3 * C), jnp.bfloat16)
+    half_gain = 0.5 * gain[...].reshape(1, C)
 
     def one(i, carry):
         values = first_out[i]
         mean = jnp.mean(values * values, axis=1, keepdims=True)
-        scaled = values * lax.rsqrt(mean + EPSILON) * gain[...]
-        conv_in[i, CT * COLS :] = shifted(scaled / (1.0 + jnp.exp(-scaled)), position)
+        half = values * lax.rsqrt(mean + EPSILON) * half_gain
+        conv_in[i, CT * COLS :] = shifted(half + half * jnp.tanh(half), position)
         return carry
 
     lax.fori_loop(0, MID, one, 0)
@@ -117,28 +145,38 @@
     )
 
 
-def tap_sum(start, base, count, time_tap, low, high, w_mid, conv_in):
-    at = (low + time_tap) * COLS
-    size = (high - low) * COLS
+def frame_sum(start, base, count, frame, frames, low, high, w_mid, conv_in):
+    at = frame * COLS
+    size = frames * COLS
     blocks = []
     for r in range(count):
         picks = tap_rows(start, base + r)
         blocks.append(
-            jnp.concatenate([conv_in[pick, at : at + size, :] for pick in picks], axis=1)
+            jnp.concatenate([conv_in[at_row, at : at + size, :] for at_row in picks], axis=1)
         )
     slab = jnp.concatenate(blocks, axis=0)
-    return jnp.dot(slab, w_mid[time_tap], preferred_element_type=jnp.float32)
+    return jnp.dot(slab, w_mid[:, low * C : high * C], preferred_element_type=jnp.float32)
+
+
+def spread_sum(base, count, frame, frames, low, high, total, first_out):
+    size = frames * COLS
+    for r in range(count):
+        for tap in range(low, high):
+            at = (frame - tap) * COLS
+            part = total[r * size : (r + 1) * size, (tap - low) * C : (tap - low + 1) * C]
+            first_out[base + r + 1, at : at + size] += part
+
+
+NEW_FRAMES = ((2, 2, 0, 3), (4, 1, 1, 3), (5, 1, 2, 3))
+OLD_FRAMES = ((1, 1, 0, 2), (0, 1, 0, 1))
 
 
 def second_new(start, w_mid, first_out, conv_in, chunk):
     def some(part, carry):
         base = part * chunk
-        for time_tap in range(3):
-            low = CT - time_tap
-            size = (F - low) * COLS
-            total = tap_sum(start, base, chunk, time_tap, low, F, w_mid, conv_in)
-            for r in range(chunk):
-                first_out[base + r + 1, low * COLS :] += total[r * size : (r + 1) * size]
+        for frame, frames, low, high in NEW_FRAMES:
+            total = frame_sum(start, base, chunk, frame, frames, low, high, w_mid, conv_in)
+            spread_sum(base, chunk, frame, frames, low, high, total, first_out)
         return carry
 
     lax.fori_loop(0, BAND // chunk, some, 0)
@@ -147,11 +185,9 @@
 def second_old(start, live, w_mid, first_out, conv_in, out, chunk):
     def some(part, carry):
         base = part * chunk
-        for time_tap in range(CT):
-            size = (CT - time_tap) * COLS
-            total = tap_sum(start, base, chunk, time_tap, 0, CT - time_tap, w_mid, conv_in)
-            for r in range(chunk):
-                first_out[base + r + 1, :size] += total[r * size : (r + 1) * size]
+        for frame, frames, low, high in OLD_FRAMES:
+            total = frame_sum(start, base, chunk, frame, frames, low, high, w_mid, conv_in)
+            spread_sum(base, chunk, frame, frames, low, high, total, first_out)
         for r in range(chunk):
             value = first_out[base + r + 1]
             out[base + r] = jnp.where(base + r < live, value, 0.0).astype(jnp.bfloat16)
@@ -163,12 +199,20 @@
 def block(
     clip_group,
     band_rows,
-    lat,
-    act,
+    new_lat,
+    old_lat,
+    old_act,
     gain,
     w_in,
     w_mid,
     out,
+    raw_new,
+    raw_old,
+    raw_act,
+    rows_lat,
+    rows_act,
+    pick,
+    pairs,
     got_lat,
     got_act,
     clip_lat,
@@ -193,7 +237,15 @@
     owners = lax.axis_size("dec")
     seq_at = lax.axis_index("seq")
     dec_at = lax.axis_index("dec")
-    per_owner = lat.shape[1]
+    per_owner = new_lat.shape[0]
+
+    raw = [
+        pltpu.make_async_copy(new_lat, raw_new, load.at[12]),
+        pltpu.make_async_copy(old_lat, raw_old, load.at[13]),
+        pltpu.make_async_copy(old_act, raw_act, load.at[14]),
+    ]
+    for copy in raw:
+        copy.start()
 
     barrier = pltpu.get_barrier_semaphore()
     for step in range(1, groups):
@@ -215,16 +267,48 @@
 
     lax.fori_loop(1, owners, greet, 0)
 
+    for copy in raw:
+        copy.wait()
+    wide = COLS * ZC
+    flat_lat = rows_lat.reshape(per_owner, wide // LANES, groups * PAD_FRAMES, LANES)
+    flat_act = rows_act.reshape(per_owner, C // LANES, groups * CT * COLS, LANES)
+    for t in range(per_owner):
+        values = raw_old[t].astype(jnp.float32)
+        for frame in range(CT):
+            at = pl.ds(frame, groups, stride=PAD_FRAMES)
+            for k in range(wide // LANES):
+                lane = frame * wide + k * LANES
+                flat_lat[t, k, at, :] = values[:, lane : lane + LANES]
+        values = raw_new[t].astype(jnp.float32)
+        for frame in range(F):
+            at = pl.ds(CT + frame, groups, stride=PAD_FRAMES)
+            for k in range(wide // LANES):
+                lane = frame * wide + k * LANES
+                flat_lat[t, k, at, :] = values[:, lane : lane + LANES]
+        for frame in range(FRAMES, PAD_FRAMES):
+            at = pl.ds(frame, groups, stride=PAD_FRAMES)
+            for k in range(wide // LANES):
+                flat_lat[t, k, at, :] = jnp.zeros((groups, LANES), jnp.float32)
+        for q in range(CT * COLS):
+            values = raw_act[t, :, q * C : (q + 1) * C].astype(jnp.float32)
+            at = pl.ds(q, groups, stride=CT * COLS)
+            for k in range(C // LANES):
+                flat_act[t, k, at, :] = values[:, k * LANES : (k + 1) * LANES]
+
     for group in range(groups):
         clip = jnp.int32(0)
         for i in range(groups):
             clip = clip + jnp.where(clip_group[seq_at, i] == group, i, 0)
         clip = jnp.minimum(clip, groups - 1)
-        clip_lat[group] = lat[clip]
-        clip_act[group] = act[clip]
+        for t in range(per_owner):
+            parts = [rows_lat[t, k, clip] for k in range(wide // LANES)]
+            clip_lat[group, t] = jnp.concatenate(parts, axis=1).astype(jnp.bfloat16)
+            parts = [rows_act[t, k, clip] for k in range(C // LANES)]
+            clip_act[group, t] = jnp.concatenate(parts, axis=1).astype(jnp.bfloat16)
     stack_lat[seq_at] = clip_lat[seq_at]
     stack_act[seq_at] = clip_act[seq_at]
     w_first[...] = jnp.zeros_like(w_first)
+    make_pick(pick)
     pl.semaphore_wait(barrier, groups - 1 + owners - 1)
 
     def to_group(step, which):
@@ -243,7 +327,12 @@
         for step in range(1, groups):
             to_group(step, which).start()
 
-    loads = [pltpu.make_async_copy(w_mid, w_second, load.at[9])]
+    loads = [
+        pltpu.make_async_copy(
+            w_mid.at[tap], w_second.at[:, tap * C : (tap + 1) * C], load.at[9 + tap]
+        )
+        for tap in range(3)
+    ]
     for time_tap in range(3):
         for row_tap in range(3):
             tap = time_tap * 3 + row_tap
@@ -253,7 +342,7 @@
                     w_in.at[tap], w_first.at[at : at + 3 * ZC, :], load.at[tap]
                 )
             )
-    for copy in loads[1:] + loads[:1]:
+    for copy in loads[3:] + loads[:3]:
         copy.start()
 
     def held_row(owner, start):
@@ -306,12 +395,13 @@
     pass_on(0)
     pass_on(1)
     collect(0)
-    for copy in loads[1:]:
+    for copy in loads[3:]:
         copy.wait()
-    first_stage(start, got_lat, spread, taps, w_first, first_out)
+    first_stage(start, got_lat, pick, pairs, spread, taps, w_first, first_out)
     act_stage(gain, first_out, conv_in)
-    loads[0].wait()
-    second_new(start, w_second, first_out, conv_in, 8)
+    for copy in loads[:3]:
+        copy.wait()
+    second_new(start, w_second, first_out, conv_in, 12)
     collect(1)
     cache_stage(start, got_act, conv_in)
     second_old(start, live, w_second, first_out, conv_in, out, 24)
@@ -327,11 +417,11 @@
         lax.fori_loop(1, owners, finish, 0)
 
 
-def run_block(clip_group, band_rows, lat, act, gain, w_in, w_mid):
+def run_block(clip_group, band_rows, new_lat, old_lat, old_act, gain, w_in, w_mid):
     groups = lax.axis_size("seq")
     owners = lax.axis_size("dec")
-    per_owner = lat.shape[1]
-    lat_row, act_row = lat.shape[2:], act.shape[2:]
+    per_owner = new_lat.shape[0]
+    lat_row, act_row = (PAD_FRAMES, COLS * ZC), (CT * COLS, C)
     bf16 = jnp.bfloat16
     vm = pl.BlockSpec(memory_space=pltpu.VMEM)
     sm = pl.BlockSpec(memory_space=pltpu.SMEM)
@@ -339,9 +429,16 @@
     return pl.pallas_call(
         block,
         out_shape=jax.ShapeDtypeStruct((BAND, ROW, C), bf16),
-        in_specs=[sm, sm, vm, vm, vm, hbm, hbm],
+        in_specs=[sm, sm, hbm, hbm, hbm, vm, hbm, hbm],
         out_specs=vm,
         scratch_shapes=[
+            pltpu.VMEM(new_lat.shape, bf16),
+            pltpu.VMEM(old_lat.shape, bf16),
+            pltpu.VMEM(old_act.shape, bf16),
+            pltpu.VMEM((per_owner, COLS * ZC // LANES, groups, PAD_FRAMES, LANES), jnp.float32),
+            pltpu.VMEM((per_owner, C // LANES, groups, CT * COLS, LANES), jnp.float32),
+            pltpu.VMEM((COLS // TOGETHER, 2 * COLS * ZC, TOGETHER * LANES), bf16),
+            pltpu.VMEM((EXT // 2, 2 * PAD_FRAMES, 2 * COLS * ZC), bf16),
             pltpu.VMEM((owners,) + lat_row, bf16),
             pltpu.VMEM((owners,) + act_row, bf16),
             pltpu.VMEM((groups, per_owner) + lat_row, bf16),
@@ -351,8 +448,8 @@
             pltpu.VMEM((owners,) + lat_row, bf16),
             pltpu.VMEM((owners,) + act_row, bf16),
             pltpu.VMEM((768, C), bf16),
-            pltpu.VMEM(w_mid.shape, bf16),
-            pltpu.VMEM((EXT + 1, PAD_FRAMES * COLS, LANES), jnp.float32),
+            pltpu.VMEM((9 * C, 3 * C), bf16),
+            pltpu.VMEM((EXT * PAD_FRAMES * COLS, LANES), jnp.float32),
             pltpu.VMEM((EXT + 1, FRAMES * COLS, LANES), bf16),
             pltpu.VMEM((MID, ROW, C), jnp.float32),
             pltpu.VMEM((MID + 1, FRAMES * COLS, 3 * C), bf16),
@@ -360,27 +457,26 @@
             pltpu.SemaphoreType.DMA((2, groups)),
             pltpu.SemaphoreType.DMA((2, owners)),
             pltpu.SemaphoreType.DMA((2, owners)),
-            pltpu.SemaphoreType.DMA((10,)),
+            pltpu.SemaphoreType.DMA((15,)),
         ],
         compiler_params=pltpu.CompilerParams(
-            collective_id=0, has_side_effects=True, vmem_limit_bytes=52 << 20
+            collective_id=0, has_side_effects=True, vmem_limit_bytes=56 << 20
         ),
         name="block",
-    )(clip_group, band_rows, lat, act, gain, w_in, w_mid)
+    )(clip_group, band_rows, new_lat, old_lat, old_act, gain, w_in, w_mid)
 
 
 def shards(latents, cache_lat, cache_act, w_in, w_mid, norm_gain, clip_group, band_rows):
-    groups, per_owner = latents.shape[1], latents.shape[2]
-    new_lat = latents.reshape(groups, per_owner, F, COLS * ZC)
-    old_lat = cache_lat.reshape(groups, per_owner, CT, COLS * ZC)
-    lat = jnp.concatenate([old_lat, new_lat, jnp.zeros_like(old_lat)], axis=2)
-    act = cache_act.reshape(groups, per_owner, CT * COLS, C)
+    def by_time(rows):
+        return jnp.transpose(rows[0, :, :, 0, :], (1, 0, 2))
+
     out = run_block(
         clip_group,
         band_rows,
-        lat,
-        act,
-        norm_gain.reshape(1, C),
+        by_time(latents),
+        by_time(cache_lat),
+        by_time(cache_act),
+        norm_gain,
         w_in.reshape(9, 3 * ZC, C),
         w_mid.reshape(3, 9 * C, C),
     )

time: 53.6 us -> 48.8 us (0.910)
  the two profiles are of different devices: /device:TPU:1 before, /device:TPU:31 now
where the time goes in v2:
time: 48.8 us; the launch traced here: 48.6 us
  Pallas kernels  46.2 us (95%)
  local copies, waits for them, and re-layouts  2.4 us (5%)
    pallas_call x1, Pallas kernels, run_block(): pl.pallas_call(block, out_shape=jax.ShapeDtypeStruct((BAND, ROW, C), bf16...  46.2 us
    unnamed x1, local copies, waits for them, and re-layouts  2.4 us

profile of v2, /device:TPU:31, one launch (start us, length us, event | category | flops | bytes accessed | tf_op | source)
XLA Modules:
  0.0 48.6 jit_solution(12857391253402909883)
XLA Ops:
  0.0 46.2 %block.1 = bf16[24,64,384]{2,1,0:T(8,128)(2,1)} custom-call(s32[4,4]{1,0:T(4,128)} %clip_group.1, s32[4,32]{1,0:T(4,128)} %band_rows.1, bf16[3,4,1024]{2,1,0:T(4,128)(2,1)} %bitcast.16, bf16[3,4,512]{2,1,0:T(4,128)(2,1)} %bitcast.17, bf16[3,4,12288]{2,1,0:T(4,128)(2,1)} %bitcast.15, f32[384]{0:T(512)} %gain.1, bf16[9,48,384]{2,1,0:T(8,128)(2,1)} %bitcast.14, ...), custom_call_target="tpu_custom_call" | custom-call | tf_op jit(solution)/shard_map/block/pallas_call | solution.py:429
  46.2 2.4 %copy.10 = bf16[1,1,24,4,16,384]{5,4,3,2,1,0:T(8,128)(2,1)} copy(bf16[1,1,24,4,16,384]{5,4,3,2,1,0:T(8,128)(2,1)} %bitcast.13) | data formatting | bytes 2359296

commit v3 on v2

--- a/solution.py
+++ b/solution.py
@@ -110,90 +110,125 @@
     return jnp.concatenate([before, values, after], axis=1).astype(jnp.bfloat16)
 
 
-def cache_stage(start, got_act, conv_in):
+HALF = BAND // 2
+SPAN = HALF + 2
+
+
+def act_row(row, gain, first_out, position):
+    values = first_out[row]
+    mean = jnp.mean(values * values, axis=1, keepdims=True)
+    half = values * lax.rsqrt(mean + EPSILON) * gain
+    return shifted(half + half * jnp.tanh(half), position)
+
+
+def act_first(gain, first_out, conv_a, conv_b):
+    position = lax.broadcasted_iota(jnp.int32, (ROW, C), 0) & (COLS - 1)
+    half_gain = 0.5 * gain[...].reshape(1, C)
+    zero = jnp.zeros((FRAMES * COLS, 3 * C), jnp.bfloat16)
+    conv_a[SPAN] = zero
+    conv_b[SPAN] = zero
+
+    def one(i, carry):
+        conv_a[i, CT * COLS :] = act_row(i, half_gain, first_out, position)
+        return carry
+
+    lax.fori_loop(0, SPAN, one, 0)
+    for i in range(2):
+        conv_b[i, CT * COLS :] = conv_a[HALF + i, CT * COLS :]
+
+
+def cache_stage(start, got_act, conv_a, conv_b):
     position = lax.broadcasted_iota(jnp.int32, (CT * COLS, C), 0) & (COLS - 1)
 
     def one(i, carry):
-        values = got_act[(start - 1 + i) & 31].astype(jnp.float32)
-        conv_in[i, : CT * COLS] = shifted(values, position)
-        return carry
-
-    lax.fori_loop(0, MID, one, 0)
-
-
-def act_stage(gain, first_out, conv_in):
-    position = lax.broadcasted_iota(jnp.int32, (ROW, C), 0) & (COLS - 1)
-    conv_in[MID] = jnp.zeros((FRAMES * COLS, 3 * C), jnp.bfloat16)
-    half_gain = 0.5 * gain[...].reshape(1, C)
-
-    def one(i, carry):
-        values = first_out[i]
-        mean = jnp.mean(values * values, axis=1, keepdims=True)
-        half = values * lax.rsqrt(mean + EPSILON) * half_gain
-        conv_in[i, CT * COLS :] = shifted(half + half * jnp.tanh(half), position)
-        return carry
-
-    lax.fori_loop(0, MID, one, 0)
-
-
-def tap_rows(start, row):
-    height = lax.rem(start + row, 96)
+        for half, conv in enumerate((conv_a, conv_b)):
+            at = start - 1 + i + half * HALF
+            values = got_act[at & 31].astype(jnp.float32)
+            conv[i, : CT * COLS] = shifted(values, position)
+        return carry
+
+    lax.fori_loop(0, SPAN, one, 0)
+
+
+def tap_rows(start, half, row):
+    height = lax.rem(start + half * HALF + row, 96)
     return (
-        jnp.where(height == 0, MID, row),
+        jnp.where(height == 0, SPAN, row),
         row + 1,
-        jnp.where(height == 95, MID, row + 2),
+        jnp.where(height == 95, SPAN, row + 2),
     )
 
 
-def frame_sum(start, base, count, frame, frames, low, high, w_mid, conv_in):
+def slab_of(start, half, frame, frames, conv_in):
     at = frame * COLS
     size = frames * COLS
     blocks = []
-    for r in range(count):
-        picks = tap_rows(start, base + r)
+    for r in range(HALF):
+        picks = tap_rows(start, half, r)
         blocks.append(
-            jnp.concatenate([conv_in[at_row, at : at + size, :] for at_row in picks], axis=1)
+            jnp.concatenate([conv_in[row, at : at + size, :] for row in picks], axis=1)
         )
-    slab = jnp.concatenate(blocks, axis=0)
-    return jnp.dot(slab, w_mid[:, low * C : high * C], preferred_element_type=jnp.float32)
-
-
-def spread_sum(base, count, frame, frames, low, high, total, first_out):
+    return jnp.concatenate(blocks, axis=0)
+
+
+def add_columns(half, frame, frames, low, left, total, first_out):
     size = frames * COLS
-    for r in range(count):
-        for tap in range(low, high):
-            at = (frame - tap) * COLS
-            part = total[r * size : (r + 1) * size, (tap - low) * C : (tap - low + 1) * C]
-            first_out[base + r + 1, at : at + size] += part
+    for piece in range(total.shape[1] // LANES):
+        column = left + piece * LANES
+        tap = low + column // C
+        at = (frame - tap) * COLS
+        lane = column % C
+        for r in range(HALF):
+            part = total[r * size : (r + 1) * size, piece * LANES : (piece + 1) * LANES]
+            first_out[half * HALF + r + 1, at : at + size, lane : lane + LANES] += part
 
 
 NEW_FRAMES = ((2, 2, 0, 3), (4, 1, 1, 3), (5, 1, 2, 3))
 OLD_FRAMES = ((1, 1, 0, 2), (0, 1, 0, 1))
 
 
-def second_new(start, w_mid, first_out, conv_in, chunk):
-    def some(part, carry):
-        base = part * chunk
-        for frame, frames, low, high in NEW_FRAMES:
-            total = frame_sum(start, base, chunk, frame, frames, low, high, w_mid, conv_in)
-            spread_sum(base, chunk, frame, frames, low, high, total, first_out)
-        return carry
-
-    lax.fori_loop(0, BAND // chunk, some, 0)
-
-
-def second_old(start, live, w_mid, first_out, conv_in, out, chunk):
-    def some(part, carry):
-        base = part * chunk
-        for frame, frames, low, high in OLD_FRAMES:
-            total = frame_sum(start, base, chunk, frame, frames, low, high, w_mid, conv_in)
-            spread_sum(base, chunk, frame, frames, low, high, total, first_out)
-        for r in range(chunk):
-            value = first_out[base + r + 1]
-            out[base + r] = jnp.where(base + r < live, value, 0.0).astype(jnp.bfloat16)
-        return carry
-
-    lax.fori_loop(0, BAND // chunk, some, 0)
+def products(start, half, groups_of, w_mid, first_out, conv_in, between=None):
+    pending = list(between or ())
+    tiles = sum(-(-(high - low) * C // 256) for _, _, low, high in groups_of)
+    done = 0
+    count = len(pending)
+    for frame, frames, low, high in groups_of:
+        slab = slab_of(start, half, frame, frames, conv_in)
+        width = (high - low) * C
+        for left in range(0, width, 256):
+            right = min(left + 256, width)
+            total = jnp.dot(
+                slab,
+                w_mid[:, low * C + left : low * C + right],
+                preferred_element_type=jnp.float32,
+            )
+            add_columns(half, frame, frames, low, left, total, first_out)
+            done += 1
+            while pending and (count - len(pending)) < count * done // tiles:
+                pending.pop(0)()
+
+
+def second_new(start, gain, w_mid, first_out, conv_a, conv_b):
+    position = lax.broadcasted_iota(jnp.int32, (ROW, C), 0) & (COLS - 1)
+    half_gain = 0.5 * gain[...].reshape(1, C)
+
+    def rest(i):
+        conv_b[i, CT * COLS :] = act_row(HALF + i, half_gain, first_out, position)
+
+    later = [lambda i=i: rest(i) for i in range(2, SPAN)]
+    products(start, 0, NEW_FRAMES, w_mid, first_out, conv_a, later)
+    products(start, 1, NEW_FRAMES, w_mid, first_out, conv_b)
+
+
+def second_old(start, live, w_mid, first_out, conv_a, conv_b, out):
+    for half, conv in enumerate((conv_a, conv_b)):
+        products(start, half, OLD_FRAMES, w_mid, first_out, conv)
+
+    def emit(r, carry):
+        out[r] = jnp.where(r < live, first_out[r + 1], 0.0).astype(jnp.bfloat16)
+        return carry
+
+    lax.fori_loop(0, BAND, emit, 0)
 
 
 def block(
@@ -226,7 +261,8 @@
     spread,
     taps,
     first_out,
-    conv_in,
+    conv_a,
+    conv_b,
     send_one,
     recv_one,
     send_two,
@@ -244,89 +280,6 @@
         pltpu.make_async_copy(old_lat, raw_old, load.at[13]),
         pltpu.make_async_copy(old_act, raw_act, load.at[14]),
     ]
-    for copy in raw:
-        copy.start()
-
-    barrier = pltpu.get_barrier_semaphore()
-    for step in range(1, groups):
-        pl.semaphore_signal(
-            barrier,
-            inc=1,
-            device_id=(lax.rem(seq_at + step, groups), dec_at),
-            device_id_type=MESH,
-        )
-
-    def greet(step, carry):
-        pl.semaphore_signal(
-            barrier,
-            inc=1,
-            device_id=(seq_at, lax.rem(dec_at + step, owners)),
-            device_id_type=MESH,
-        )
-        return carry
-
-    lax.fori_loop(1, owners, greet, 0)
-
-    for copy in raw:
-        copy.wait()
-    wide = COLS * ZC
-    flat_lat = rows_lat.reshape(per_owner, wide // LANES, groups * PAD_FRAMES, LANES)
-    flat_act = rows_act.reshape(per_owner, C // LANES, groups * CT * COLS, LANES)
-    for t in range(per_owner):
-        values = raw_old[t].astype(jnp.float32)
-        for frame in range(CT):
-            at = pl.ds(frame, groups, stride=PAD_FRAMES)
-            for k in range(wide // LANES):
-                lane = frame * wide + k * LANES
-                flat_lat[t, k, at, :] = values[:, lane : lane + LANES]
-        values = raw_new[t].astype(jnp.float32)
-        for frame in range(F):
-            at = pl.ds(CT + frame, groups, stride=PAD_FRAMES)
-            for k in range(wide // LANES):
-                lane = frame * wide + k * LANES
-                flat_lat[t, k, at, :] = values[:, lane : lane + LANES]
-        for frame in range(FRAMES, PAD_FRAMES):
-            at = pl.ds(frame, groups, stride=PAD_FRAMES)
-            for k in range(wide // LANES):
-                flat_lat[t, k, at, :] = jnp.zeros((groups, LANES), jnp.float32)
-        for q in range(CT * COLS):
-            values = raw_act[t, :, q * C : (q + 1) * C].astype(jnp.float32)
-            at = pl.ds(q, groups, stride=CT * COLS)
-            for k in range(C // LANES):
-                flat_act[t, k, at, :] = values[:, k * LANES : (k + 1) * LANES]
-
-    for group in range(groups):
-        clip = jnp.int32(0)
-        for i in range(groups):
-            clip = clip + jnp.where(clip_group[seq_at, i] == group, i, 0)
-        clip = jnp.minimum(clip, groups - 1)
-        for t in range(per_owner):
-            parts = [rows_lat[t, k, clip] for k in range(wide // LANES)]
-            clip_lat[group, t] = jnp.concatenate(parts, axis=1).astype(jnp.bfloat16)
-            parts = [rows_act[t, k, clip] for k in range(C // LANES)]
-            clip_act[group, t] = jnp.concatenate(parts, axis=1).astype(jnp.bfloat16)
-    stack_lat[seq_at] = clip_lat[seq_at]
-    stack_act[seq_at] = clip_act[seq_at]
-    w_first[...] = jnp.zeros_like(w_first)
-    make_pick(pick)
-    pl.semaphore_wait(barrier, groups - 1 + owners - 1)
-
-    def to_group(step, which):
-        group = lax.rem(seq_at + step, groups)
-        source, target = ((clip_lat, stack_lat), (clip_act, stack_act))[which]
-        return pltpu.make_async_remote_copy(
-            src_ref=source.at[group],
-            dst_ref=target.at[seq_at],
-            send_sem=send_one.at[which, step],
-            recv_sem=recv_one.at[which, step],
-            device_id=(group, dec_at),
-            device_id_type=MESH,
-        )
-
-    for which in range(2):
-        for step in range(1, groups):
-            to_group(step, which).start()
-
     loads = [
         pltpu.make_async_copy(
             w_mid.at[tap], w_second.at[:, tap * C : (tap + 1) * C], load.at[9 + tap]
@@ -342,8 +295,99 @@
                     w_in.at[tap], w_first.at[at : at + 3 * ZC, :], load.at[tap]
                 )
             )
-    for copy in loads[3:] + loads[:3]:
+    for copy in raw + loads[:3]:
         copy.start()
+
+    barrier = pltpu.get_barrier_semaphore()
+    for step in range(1, groups):
+        pl.semaphore_signal(
+            barrier,
+            inc=1,
+            device_id=(lax.rem(seq_at + step, groups), dec_at),
+            device_id_type=MESH,
+        )
+
+    def greet(step, carry):
+        pl.semaphore_signal(
+            barrier,
+            inc=1,
+            device_id=(seq_at, lax.rem(dec_at + step, owners)),
+            device_id_type=MESH,
+        )
+        return carry
+
+    lax.fori_loop(1, owners, greet, 0)
+
+    for copy in raw[:2]:
+        copy.wait()
+    wide = COLS * ZC
+    flat_lat = rows_lat.reshape(per_owner, wide // LANES, groups * PAD_FRAMES, LANES)
+    flat_act = rows_act.reshape(per_owner, C // LANES, groups * CT * COLS, LANES)
+    for t in range(per_owner):
+        old = raw_old[t].astype(jnp.float32)
+        new = raw_new[t].astype(jnp.float32)
+        for frame in range(PAD_FRAMES):
+            at = pl.ds(frame, groups, stride=PAD_FRAMES)
+            for k in range(wide // LANES):
+                lane = frame * wide + k * LANES
+                if frame < CT:
+                    values = old[:, lane : lane + LANES]
+                elif frame < FRAMES:
+                    lane -= CT * wide
+                    values = new[:, lane : lane + LANES]
+                else:
+                    values = jnp.zeros((groups, LANES), jnp.float32)
+                flat_lat[t, k, at, :] = values
+
+    clips = []
+    for group in range(groups):
+        clip = jnp.int32(0)
+        for i in range(groups):
+            clip = clip + jnp.where(clip_group[seq_at, i] == group, i, 0)
+        clips.append(jnp.minimum(clip, groups - 1))
+
+    def by_group(rows, target, stack):
+        for group in range(groups):
+            for t in range(per_owner):
+                parts = [rows[t, k, clips[group]] for k in range(rows.shape[1])]
+                target[group, t] = jnp.concatenate(parts, axis=1).astype(jnp.bfloat16)
+        stack[seq_at] = target[seq_at]
+
+    by_group(rows_lat, clip_lat, stack_lat)
+    pl.semaphore_wait(barrier, groups - 1 + owners - 1)
+
+    def to_group(step, which):
+        group = lax.rem(seq_at + step, groups)
+        source, target = ((clip_lat, stack_lat), (clip_act, stack_act))[which]
+        return pltpu.make_async_remote_copy(
+            src_ref=source.at[group],
+            dst_ref=target.at[seq_at],
+            send_sem=send_one.at[which, step],
+            recv_sem=recv_one.at[which, step],
+            device_id=(group, dec_at),
+            device_id_type=MESH,
+        )
+
+    for step in range(1, groups):
+        to_group(step, 0).start()
+
+    raw[2].wait()
+    for t in range(per_owner):
+        for q in range(CT * COLS):
+            at = pl.ds(q, groups, stride=CT * COLS)
+            for k in range(C // LANES):
+                lane = q * C + k * LANES
+                values = raw_act[t, :, lane : lane + LANES].astype(jnp.float32)
+                flat_act[t, k, at, :] = values
+    by_group(rows_act, clip_act, stack_act)
+    for step in range(1, groups):
+        to_group(step, 1).start()
+
+    w_first[...] = jnp.zeros_like(w_first)
+    for copy in loads[3:]:
+        copy.start()
+    make_pick(pick)
+
 
     def held_row(owner, start):
         first = lax.shift_right_arithmetic(start - 2 - dec_at + owners - 1, 5)
@@ -361,7 +405,7 @@
             device_id_type=MESH,
         )
 
-    def pass_on(which):
+    def fill(which):
         stack, slot, got = (
             (stack_lat, slot_lat, got_lat),
             (stack_act, slot_act, got_act),
@@ -369,14 +413,15 @@
         for step in range(1, groups):
             to_group(step, which).wait_recv()
 
-        def fill(owner, start):
+        def one(owner, start):
             row = held_row(owner, start)
             slot[owner] = stack[row // per_owner, lax.rem(row, per_owner)]
             return start + band_rows[seq_at, owner]
 
-        lax.fori_loop(0, owners, fill, jnp.int32(0))
+        lax.fori_loop(0, owners, one, jnp.int32(0))
         got[dec_at] = slot[dec_at]
 
+    def pass_on(which):
         def launch(step, carry):
             to_owner(step, which).start()
             return carry
@@ -392,19 +437,21 @@
 
     start = band_start(band_rows, seq_at, dec_at, owners)
     live = band_rows[seq_at, dec_at]
+    fill(0)
     pass_on(0)
+    fill(1)
+    collect(0)
     pass_on(1)
-    collect(0)
     for copy in loads[3:]:
         copy.wait()
     first_stage(start, got_lat, pick, pairs, spread, taps, w_first, first_out)
-    act_stage(gain, first_out, conv_in)
+    act_first(gain, first_out, conv_a, conv_b)
     for copy in loads[:3]:
         copy.wait()
-    second_new(start, w_second, first_out, conv_in, 12)
+    second_new(start, gain, w_second, first_out, conv_a, conv_b)
     collect(1)
-    cache_stage(start, got_act, conv_in)
-    second_old(start, live, w_second, first_out, conv_in, out, 24)
+    cache_stage(start, got_act, conv_a, conv_b)
+    second_old(start, live, w_second, first_out, conv_a, conv_b, out)
 
     for which in range(2):
         for step in range(1, groups):
@@ -452,7 +499,8 @@
             pltpu.VMEM((EXT * PAD_FRAMES * COLS, LANES), jnp.float32),
             pltpu.VMEM((EXT + 1, FRAMES * COLS, LANES), bf16),
             pltpu.VMEM((MID, ROW, C), jnp.float32),
-            pltpu.VMEM((MID + 1, FRAMES * COLS, 3 * C), bf16),
+            pltpu.VMEM((SPAN + 1, FRAMES * COLS, 3 * C), bf16),
+            pltpu.VMEM((SPAN + 1, FRAMES * COLS, 3 * C), bf16),
             pltpu.SemaphoreType.DMA((2, groups)),
             pltpu.SemaphoreType.DMA((2, groups)),
             pltpu.SemaphoreType.DMA((2, owners)),

time: 48.8 us -> 46.3 us (0.949)
  the two profiles are of different devices: /device:TPU:31 before, /device:TPU:1 now
where the time goes in v3:
time: 46.3 us; the launch traced here: 46.1 us
  Pallas kernels  43.7 us (94%)
  local copies, waits for them, and re-layouts  2.4 us (5%)
    pallas_call x1, Pallas kernels, run_block(): pl.pallas_call(block, out_shape=jax.ShapeDtypeStruct((BAND, ROW, C), bf16...  43.7 us
    unnamed x1, local copies, waits for them, and re-layouts  2.4 us

profile of v3, /device:TPU:1, one launch (start us, length us, event | category | flops | bytes accessed | tf_op | source)
XLA Modules:
  0.0 46.1 jit_solution(11794826452414278205)
XLA Ops:
  0.0 43.7 %block.1 = bf16[24,64,384]{2,1,0:T(8,128)(2,1)} custom-call(s32[4,4]{1,0:T(4,128)} %clip_group.1, s32[4,32]{1,0:T(4,128)} %band_rows.1, bf16[3,4,1024]{2,1,0:T(4,128)(2,1)} %bitcast.16, bf16[3,4,512]{2,1,0:T(4,128)(2,1)} %bitcast.17, bf16[3,4,12288]{2,1,0:T(4,128)(2,1)} %bitcast.15, f32[384]{0:T(512)} %gain.1, bf16[9,48,384]{2,1,0:T(8,128)(2,1)} %bitcast.14, ...), custom_call_target="tpu_custom_call" | custom-call | tf_op jit(solution)/shard_map/block/pallas_call | solution.py:476
  43.7 2.4 %copy.10 = bf16[1,1,24,4,16,384]{5,4,3,2,1,0:T(8,128)(2,1)} copy(bf16[1,1,24,4,16,384]{5,4,3,2,1,0:T(8,128)(2,1)} %bitcast.13) | data formatting | bytes 2359296

commit v4 on v3

--- a/solution.py
+++ b/solution.py
@@ -204,7 +204,7 @@
             )
             add_columns(half, frame, frames, low, left, total, first_out)
             done += 1
-            while pending and (count - len(pending)) < count * done // tiles:
+            while pending and (count - len(pending)) < -(-count * done // tiles):
                 pending.pop(0)()
 
 
@@ -220,15 +220,18 @@
     products(start, 1, NEW_FRAMES, w_mid, first_out, conv_b)
 
 
-def second_old(start, live, w_mid, first_out, conv_a, conv_b, out):
-    for half, conv in enumerate((conv_a, conv_b)):
-        products(start, half, OLD_FRAMES, w_mid, first_out, conv)
-
-    def emit(r, carry):
+def second_old(start, live, w_mid, first_out, conv_a, conv_b, out, leave):
+    def emit(r):
         out[r] = jnp.where(r < live, first_out[r + 1], 0.0).astype(jnp.bfloat16)
-        return carry
-
-    lax.fori_loop(0, BAND, emit, 0)
+
+    def emit_half(half):
+        for r in range(half * HALF, (half + 1) * HALF):
+            emit(r)
+        leave(half)
+
+    products(start, 0, OLD_FRAMES, w_mid, first_out, conv_a)
+    products(start, 1, OLD_FRAMES, w_mid, first_out, conv_b, [lambda: emit_half(0)])
+    emit_half(1)
 
 
 def block(
@@ -241,6 +244,7 @@
     w_in,
     w_mid,
     out,
+    staged,
     raw_new,
     raw_old,
     raw_act,
@@ -399,8 +403,8 @@
         return pltpu.make_async_remote_copy(
             src_ref=source.at[owner],
             dst_ref=target.at[dec_at],
-            send_sem=send_two.at[which, step],
-            recv_sem=recv_two.at[which, step],
+            send_sem=send_two.at[which],
+            recv_sem=recv_two.at[which],
             device_id=(seq_at, owner),
             device_id_type=MESH,
         )
@@ -428,19 +432,24 @@
 
         lax.fori_loop(1, owners, launch, 0)
 
-    def collect(which):
-        def arrive(step, carry):
-            to_owner(step, which).wait_recv()
-            return carry
-
-        lax.fori_loop(1, owners, arrive, 0)
+    def all_owners(which):
+        source, target = ((slot_lat, got_lat), (slot_act, got_act))[which]
+        rows = pl.ds(0, owners - 1)
+        return pltpu.make_async_remote_copy(
+            src_ref=source.at[rows],
+            dst_ref=target.at[rows],
+            send_sem=send_two.at[which],
+            recv_sem=recv_two.at[which],
+            device_id=(seq_at, lax.rem(dec_at + 1, owners)),
+            device_id_type=MESH,
+        )
 
     start = band_start(band_rows, seq_at, dec_at, owners)
     live = band_rows[seq_at, dec_at]
     fill(0)
     pass_on(0)
     fill(1)
-    collect(0)
+    all_owners(0).wait_recv()
     pass_on(1)
     for copy in loads[3:]:
         copy.wait()
@@ -449,19 +458,30 @@
     for copy in loads[:3]:
         copy.wait()
     second_new(start, gain, w_second, first_out, conv_a, conv_b)
-    collect(1)
+    all_owners(1).wait_recv()
     cache_stage(start, got_act, conv_a, conv_b)
-    second_old(start, live, w_second, first_out, conv_a, conv_b, out)
+
+    def leaving(half):
+        rows = pl.ds(half * HALF, HALF)
+        return pltpu.make_async_copy(staged.at[rows], out.at[rows], load.at[15 + half])
+
+    second_old(
+        start,
+        live,
+        w_second,
+        first_out,
+        conv_a,
+        conv_b,
+        staged,
+        lambda half: leaving(half).start(),
+    )
 
     for which in range(2):
         for step in range(1, groups):
             to_group(step, which).wait_send()
-
-        def finish(step, carry, which=which):
-            to_owner(step, which).wait_send()
-            return carry
-
-        lax.fori_loop(1, owners, finish, 0)
+        all_owners(which).wait_send()
+    for half in range(2):
+        leaving(half).wait()
 
 
 def run_block(clip_group, band_rows, new_lat, old_lat, old_act, gain, w_in, w_mid):
@@ -477,8 +497,9 @@
         block,
         out_shape=jax.ShapeDtypeStruct((BAND, ROW, C), bf16),
         in_specs=[sm, sm, hbm, hbm, hbm, vm, hbm, hbm],
-        out_specs=vm,
+        out_specs=hbm,
         scratch_shapes=[
+            pltpu.VMEM((BAND, ROW, C), bf16),
             pltpu.VMEM(new_lat.shape, bf16),
             pltpu.VMEM(old_lat.shape, bf16),
             pltpu.VMEM(old_act.shape, bf16),
@@ -503,9 +524,9 @@
             pltpu.VMEM((SPAN + 1, FRAMES * COLS, 3 * C), bf16),
             pltpu.SemaphoreType.DMA((2, groups)),
             pltpu.SemaphoreType.DMA((2, groups)),
-            pltpu.SemaphoreType.DMA((2, owners)),
-            pltpu.SemaphoreType.DMA((2, owners)),
-            pltpu.SemaphoreType.DMA((15,)),
+            pltpu.SemaphoreType.DMA((2,)),
+            pltpu.SemaphoreType.DMA((2,)),
+            pltpu.SemaphoreType.DMA((17,)),
         ],
         compiler_params=pltpu.CompilerParams(
             collective_id=0, has_side_effects=True, vmem_limit_bytes=56 << 20

time: 46.3 us -> 43.7 us (0.944)
  Pallas kernels: 43.7 us -> 41.1 us
    pallas_call x1, Pallas kernels: 43.7 us -> 41.1 us  [run_block(): pl.pallas_call(block, out_shape=jax.ShapeDtypeStruct((BAND, ROW, C), bf16...]
where the time goes in v4:
time: 43.7 us; the launch traced here: 43.5 us
  Pallas kernels  41.1 us (94%)
  local copies, waits for them, and re-layouts  2.4 us (5%)
    pallas_call x1, Pallas kernels, run_block(): pl.pallas_call(block, out_shape=jax.ShapeDtypeStruct((BAND, ROW, C), bf16...  41.1 us
    unnamed x1, local copies, waits for them, and re-layouts  2.4 us

profile of v4, /device:TPU:1, one launch (start us, length us, event | category | flops | bytes accessed | tf_op | source)
XLA Modules:
  0.0 43.5 jit_solution(4577184391725186573)
XLA Ops:
  0.0 41.1 %block.1 = bf16[24,64,384]{2,1,0:T(8,128)(2,1)} custom-call(s32[4,4]{1,0:T(4,128)} %clip_group.1, s32[4,32]{1,0:T(4,128)} %band_rows.1, bf16[3,4,1024]{2,1,0:T(4,128)(2,1)} %bitcast.16, bf16[3,4,512]{2,1,0:T(4,128)(2,1)} %bitcast.17, bf16[3,4,12288]{2,1,0:T(4,128)(2,1)} %bitcast.15, f32[384]{0:T(512)} %gain.1, bf16[9,48,384]{2,1,0:T(8,128)(2,1)} %bitcast.14, ...), custom_call_target="tpu_custom_call" | custom-call | tf_op jit(solution)/shard_map/block/pallas_call | solution.py:496
  41.1 2.4 %copy.10 = bf16[1,1,24,4,16,384]{5,4,3,2,1,0:T(8,128)(2,1)} copy(bf16[1,1,24,4,16,384]{5,4,3,2,1,0:T(8,128)(2,1)} %bitcast.13) | data formatting | bytes 2359296

commit v5 on v4

--- a/solution.py
+++ b/solution.py
@@ -61,7 +61,7 @@
         pairs[i] = jnp.concatenate(rows, axis=0).astype(jnp.bfloat16)
         return carry
 
-    lax.fori_loop(0, EXT // 2, gather, 0)
+    lax.fori_loop(0, EXT // 2, gather, 0, unroll=7)
     source = pairs[...].reshape(EXT * PAD_FRAMES, 2 * COLS * ZC)
 
     def columns(part, carry):
@@ -72,7 +72,7 @@
             spread[rows, :] = block[:, i * LANES : (i + 1) * LANES]
         return carry
 
-    lax.fori_loop(0, COLS // TOGETHER, columns, 0)
+    lax.fori_loop(0, COLS // TOGETHER, columns, 0, unroll=True)
     taps[EXT] = jnp.zeros((FRAMES * COLS, LANES), jnp.bfloat16)
 
     def narrow(j, carry):
@@ -80,7 +80,7 @@
         taps[j] = spread[pl.ds(at, FRAMES * COLS), :].astype(jnp.bfloat16)
         return carry
 
-    lax.fori_loop(0, EXT, narrow, 0)
+    lax.fori_loop(0, EXT, narrow, 0, unroll=7)
 
     rows = MID // 2
     for part in range(2):
@@ -132,7 +132,7 @@
         conv_a[i, CT * COLS :] = act_row(i, half_gain, first_out, position)
         return carry
 
-    lax.fori_loop(0, SPAN, one, 0)
+    lax.fori_loop(0, SPAN, one, 0, unroll=7)
     for i in range(2):
         conv_b[i, CT * COLS :] = conv_a[HALF + i, CT * COLS :]
 
@@ -147,7 +147,7 @@
             conv[i, : CT * COLS] = shifted(values, position)
         return carry
 
-    lax.fori_loop(0, SPAN, one, 0)
+    lax.fori_loop(0, SPAN, one, 0, unroll=7)
 
 
 def tap_rows(start, half, row):
@@ -398,7 +398,7 @@
         return jnp.clip(first, 0, groups * per_owner - 1)
 
     def to_owner(step, which):
-        owner = lax.rem(dec_at + step, owners)
+        owner = lax.rem(dec_at + 1 + lax.rem(step + 9, owners - 1), owners)
         source, target = ((slot_lat, got_lat), (slot_act, got_act))[which]
         return pltpu.make_async_remote_copy(
             src_ref=source.at[owner],
@@ -422,7 +422,7 @@
             slot[owner] = stack[row // per_owner, lax.rem(row, per_owner)]
             return start + band_rows[seq_at, owner]
 
-        lax.fori_loop(0, owners, one, jnp.int32(0))
+        lax.fori_loop(0, owners, one, jnp.int32(0), unroll=4)
         got[dec_at] = slot[dec_at]
 
     def pass_on(which):
@@ -430,7 +430,7 @@
             to_owner(step, which).start()
             return carry
 
-        lax.fori_loop(1, owners, launch, 0)
+        lax.fori_loop(1, owners, launch, 0, unroll=True)
 
     def all_owners(which):
         source, target = ((slot_lat, got_lat), (slot_act, got_act))[which]

time: 43.7 us -> 41 us (0.938)
  Pallas kernels: 41.1 us -> 38.4 us
    pallas_call x1, Pallas kernels: 41.1 us -> 38.4 us  [run_block(): pl.pallas_call(block, out_shape=jax.ShapeDtypeStruct((BAND, ROW, C), bf16...]
where the time goes in v5:
time: 41 us; the launch traced here: 40.9 us
  Pallas kernels  38.4 us (94%)
  local copies, waits for them, and re-layouts  2.4 us (6%)
    pallas_call x1, Pallas kernels, run_block(): pl.pallas_call(block, out_shape=jax.ShapeDtypeStruct((BAND, ROW, C), bf16...  38.4 us
    unnamed x1, local copies, waits for them, and re-layouts  2.4 us

profile of v5, /device:TPU:1, one launch (start us, length us, event | category | flops | bytes accessed | tf_op | source)
XLA Modules:
  0.0 40.9 jit_solution(5789813297410232537)
XLA Ops:
  0.0 38.4 %block.1 = bf16[24,64,384]{2,1,0:T(8,128)(2,1)} custom-call(s32[4,4]{1,0:T(4,128)} %clip_group.1, s32[4,32]{1,0:T(4,128)} %band_rows.1, bf16[3,4,1024]{2,1,0:T(4,128)(2,1)} %bitcast.16, bf16[3,4,512]{2,1,0:T(4,128)(2,1)} %bitcast.17, bf16[3,4,12288]{2,1,0:T(4,128)(2,1)} %bitcast.15, f32[384]{0:T(512)} %gain.1, bf16[9,48,384]{2,1,0:T(8,128)(2,1)} %bitcast.14, ...), custom_call_target="tpu_custom_call" | custom-call | tf_op jit(solution)/shard_map/block/pallas_call | solution.py:496
  38.5 2.4 %copy.10 = bf16[1,1,24,4,16,384]{5,4,3,2,1,0:T(8,128)(2,1)} copy(bf16[1,1,24,4,16,384]{5,4,3,2,1,0:T(8,128)(2,1)} %bitcast.13) | data formatting | bytes 2359296

commit v6 on v5

--- a/solution.py
+++ b/solution.py
@@ -315,7 +315,7 @@
         pl.semaphore_signal(
             barrier,
             inc=1,
-            device_id=(seq_at, lax.rem(dec_at + step, owners)),
+            device_id=(seq_at, lax.rem(dec_at + 1 + lax.rem(step + 9, owners - 1), owners)),
             device_id_type=MESH,
         )
         return carry
@@ -372,7 +372,7 @@
             device_id_type=MESH,
         )
 
-    for step in range(1, groups):
+    for step in (2, 1, 3):
         to_group(step, 0).start()
 
     raw[2].wait()

time: 41 us -> 40.7 us (level)
  no operation moved by 1% of the time
where the time goes in v6:
time: 40.7 us; the launch traced here: 40.5 us
  Pallas kernels  38.1 us (94%)
  local copies, waits for them, and re-layouts  2.4 us (6%)
    pallas_call x1, Pallas kernels, run_block(): pl.pallas_call(block, out_shape=jax.ShapeDtypeStruct((BAND, ROW, C), bf16...  38.1 us
    unnamed x1, local copies, waits for them, and re-layouts  2.4 us

profile of v6, /device:TPU:1, one launch (start us, length us, event | category | flops | bytes accessed | tf_op | source)
XLA Modules:
  0.0 40.5 jit_solution(7155131270441069111)
XLA Ops:
  0.0 38.1 %block.1 = bf16[24,64,384]{2,1,0:T(8,128)(2,1)} custom-call(s32[4,4]{1,0:T(4,128)} %clip_group.1, s32[4,32]{1,0:T(4,128)} %band_rows.1, bf16[3,4,1024]{2,1,0:T(4,128)(2,1)} %bitcast.16, bf16[3,4,512]{2,1,0:T(4,128)(2,1)} %bitcast.17, bf16[3,4,12288]{2,1,0:T(4,128)(2,1)} %bitcast.15, f32[384]{0:T(512)} %gain.1, bf16[9,48,384]{2,1,0:T(8,128)(2,1)} %bitcast.14, ...), custom_call_target="tpu_custom_call" | custom-call | tf_op jit(solution)/shard_map/block/pallas_call | solution.py:496
  38.1 2.4 %copy.10 = bf16[1,1,24,4,16,384]{5,4,3,2,1,0:T(8,128)(2,1)} copy(bf16[1,1,24,4,16,384]{5,4,3,2,1,0:T(8,128)(2,1)} %bitcast.13) | data formatting | bytes 2359296

commit v7 on v6

--- a/solution.py
+++ b/solution.py
@@ -80,7 +80,7 @@
         taps[j] = spread[pl.ds(at, FRAMES * COLS), :].astype(jnp.bfloat16)
         return carry
 
-    lax.fori_loop(0, EXT, narrow, 0, unroll=7)
+    lax.fori_loop(0, EXT, narrow, 0, unroll=True)
 
     rows = MID // 2
     for part in range(2):
@@ -132,7 +132,7 @@
         conv_a[i, CT * COLS :] = act_row(i, half_gain, first_out, position)
         return carry
 
-    lax.fori_loop(0, SPAN, one, 0, unroll=7)
+    lax.fori_loop(0, SPAN, one, 0, unroll=True)
     for i in range(2):
         conv_b[i, CT * COLS :] = conv_a[HALF + i, CT * COLS :]
 

time: 40.7 us -> 39.9 us (0.980)
  Pallas kernels: 38.1 us -> 37.3 us
    pallas_call x1, Pallas kernels: 38.1 us -> 37.3 us  [run_block(): pl.pallas_call(block, out_shape=jax.ShapeDtypeStruct((BAND, ROW, C), bf16...]
where the time goes in v7:
time: 39.9 us; the launch traced here: 39.8 us
  Pallas kernels  37.3 us (93%)
  local copies, waits for them, and re-layouts  2.4 us (6%)
    pallas_call x1, Pallas kernels, run_block(): pl.pallas_call(block, out_shape=jax.ShapeDtypeStruct((BAND, ROW, C), bf16...  37.3 us
    unnamed x1, local copies, waits for them, and re-layouts  2.4 us

profile of v7, /device:TPU:1, one launch (start us, length us, event | category | flops | bytes accessed | tf_op | source)
XLA Modules:
  0.0 39.8 jit_solution(10570008002732347384)
XLA Ops:
  0.0 37.3 %block.1 = bf16[24,64,384]{2,1,0:T(8,128)(2,1)} custom-call(s32[4,4]{1,0:T(4,128)} %clip_group.1, s32[4,32]{1,0:T(4,128)} %band_rows.1, bf16[3,4,1024]{2,1,0:T(4,128)(2,1)} %bitcast.16, bf16[3,4,512]{2,1,0:T(4,128)(2,1)} %bitcast.17, bf16[3,4,12288]{2,1,0:T(4,128)(2,1)} %bitcast.15, f32[384]{0:T(512)} %gain.1, bf16[9,48,384]{2,1,0:T(8,128)(2,1)} %bitcast.14, ...), custom_call_target="tpu_custom_call" | custom-call | tf_op jit(solution)/shard_map/block/pallas_call | solution.py:496
  37.4 2.4 %copy.10 = bf16[1,1,24,4,16,384]{5,4,3,2,1,0:T(8,128)(2,1)} copy(bf16[1,1,24,4,16,384]{5,4,3,2,1,0:T(8,128)(2,1)} %bitcast.13) | data formatting | bytes 2359296
